TPU v7x, 128 devices: a whole 4x4x4 slice. The times are simulated.
128 devices in a mesh: section: 8 (over y, core), tp: 16 (over x, z).
Axes of the slice: x: 4, y: 4, z: 4, core: 2. Of those that a mesh axis runs over, the one named last changes fastest.
Arguments:
- stream_in: bfloat16 [512, 8192], P(None, 'tp')
- layer_delta: bfloat16 [8, 512, 8192], P('section', None, 'tp')
- norm_gain: float32 [8192], P('tp'), may hold values from 0.25 to 1.75
- out_embed: bfloat16 [8192, 16384], P(None, 'tp')
- exit_blocks: int32 [8, 4], P('section'), may hold values from 0 to 3
- exit_counts: int32 [8], P('section'), may hold values from 1 to 4, 16 in all
- targets: int32 [512], replicated, may hold values from 0 to 16383
Outputs:
- exit_loss: float32 [8, 4, 128], P('section')
Inputs may be any that keep to these rules, and one draw needn't show every extreme that they name: `exit_counts`: each section scores at least one block, the counts of all sections sum to 2 times the number of sections, and some section scores exactly 4. `exit_blocks`: block numbers of the micro-batch's 128-row blocks; only a section's first exit_counts entries are used.
All inputs are finite; a program needn't handle non-finite values.
Results may differ from a plain program's by a relative error of at most 0.02.
Values may be sent and summed in bfloat16 or wider, within the bound.
A program may use at most 128 MiB of HBM per device.

v0:
```python
import jax
import jax.numpy as jnp
from jax import lax
from jax.sharding import PartitionSpec as P

BLK = 128
MAXB = 4
EPS = 1e-05


def prefix(shard, axis, join, neutral):
    place = lax.axis_index(axis)
    gathered = lax.all_gather(shard.astype(jnp.bfloat16), axis)
    state = jnp.zeros_like(shard) + jnp.asarray(neutral, shard.dtype)

    def one(lap, state):
        return join(state, lax.dynamic_index_in_dim(gathered, lap, 0, False).astype(shard.dtype))

    return lax.fori_loop(0, place, one, state)


def from_root(shard, axis, root):
    mine = lax.axis_index(axis) == root
    return lax.psum(jnp.where(mine, shard, jnp.zeros_like(shard)), axis)


def add_terms(first, second):
    return first + second


def row_losses(exit_rows, teach_rows, target_rows, norm_gain, out_embed):
    width = out_embed.shape[0]
    squares = lax.psum(
        (jnp.sum(exit_rows * exit_rows, axis=1), jnp.sum(teach_rows * teach_rows, axis=1)), "tp"
    )
    normed_exit = (
        exit_rows * lax.rsqrt(squares[0] / width + EPS)[:, None] * norm_gain[None, :]
    ).astype(jnp.bfloat16)
    normed_teach = (
        teach_rows * lax.rsqrt(squares[1] / width + EPS)[:, None] * norm_gain[None, :]
    ).astype(jnp.bfloat16)
    vocab_part = out_embed.shape[1]
    logit_exit = jnp.dot(
        lax.all_gather(normed_exit, "tp", axis=1, tiled=True),
        out_embed,
        preferred_element_type=jnp.float32,
    )
    logit_teach = jnp.dot(
        lax.all_gather(normed_teach, "tp", axis=1, tiled=True),
        out_embed,
        preferred_element_type=jnp.float32,
    )
    first_column = lax.axis_index("tp") * vocab_part
    columns = jnp.arange(vocab_part, dtype=jnp.int32)
    hit = (target_rows - first_column)[:, None] == columns[None, :]
    target_part = jnp.sum(jnp.where(hit, logit_exit, 0.0), axis=1)
    peak_exit, peak_teach = lax.pmax(
        (jnp.max(logit_exit, axis=1), jnp.max(logit_teach, axis=1)), "tp"
    )
    weight_teach = jnp.exp(logit_teach - peak_teach[:, None])
    total_exit, total_teach, cross, picked = lax.psum(
        (
            jnp.sum(jnp.exp(logit_exit - peak_exit[:, None]), axis=1),
            jnp.sum(weight_teach, axis=1),
            jnp.sum(weight_teach * (logit_teach - logit_exit), axis=1),
            target_part,
        ),
        "tp",
    )
    log_exit = jnp.log(total_exit) + peak_exit
    log_teach = jnp.log(total_teach) + peak_teach
    return 2.0 * log_exit - picked + cross / total_teach - log_teach


def body(stream_in, layer_delta, norm_gain, out_embed, exit_blocks, exit_counts, targets):
    stream = stream_in.astype(jnp.float32)
    mine_delta = layer_delta[0].astype(jnp.float32)
    before = prefix(mine_delta, "section", add_terms, jnp.zeros_like(mine_delta))
    exit_all = stream + before + mine_delta
    final_all = from_root(
        exit_all.astype(jnp.bfloat16), "section", lax.axis_size("section") - 1
    ).astype(exit_all.dtype)
    starts = [exit_blocks[0, slot_index] * BLK for slot_index in range(MAXB)]
    exit_rows = jnp.concatenate(
        [lax.dynamic_slice_in_dim(exit_all, start, BLK, 0) for start in starts], axis=0
    )
    teach_rows = jnp.concatenate(
        [lax.dynamic_slice_in_dim(final_all, start, BLK, 0) for start in starts], axis=0
    )
    target_rows = jnp.concatenate(
        [lax.dynamic_slice_in_dim(targets, start, BLK, 0) for start in starts], axis=0
    )
    losses = row_losses(exit_rows, teach_rows, target_rows, norm_gain, out_embed).reshape(MAXB, BLK)
    keep = jnp.arange(MAXB, dtype=jnp.int32) < exit_counts[0]
    return jnp.where(keep[:, None], losses, 0.0)[None]


def solution(mesh):
    placed = (
        P(None, "tp"),
        P("section", None, "tp"),
        P("tp"),
        P(None, "tp"),
        P("section", None),
        P("section"),
        P(),
    )
    return jax.shard_map(
        body, mesh=mesh, in_specs=placed, out_specs=P("section", None, None), check_vma=False
    )
```

profile of v0, /device:TPU:0, one launch (start us, length us, event | category | flops | bytes accessed | tf_op | source)
XLA Modules:
  0.0 407.7 jit_solution(8671719075948042999)
XLA Ops:
  6.5 0.7 all-gather.4.cloned.1.call-update
  7.3 36.3 %all-gather.4.cloned.1.call-done = bf16[8,512,512]{2,1,0:T(8,128)(2,1)} async-done(((bf16[1,512,512]{2,1,0:T(8,128)(2,1)}), bf16[8,512,512]{2,1,0:T(8,128)(2,1)}) %all-gather.4.cloned.1.call-update) | async-done | bytes 4194320 | tf_op jit(solution)/shard_map/all_gather | solution.py:13
  43.6 0.1 broadcast_in_dim.21
  43.8 1.0 copy-done
  44.8 0.3 copy-done.1
  45.1 1.1 convert_select_fusion
  46.2 0.7 fusion.3
  49.5 0.1 constant_dynamic-slice_fusion.7
  49.6 0.1 multiply_reduce_fusion.2
  49.8 64.8 %all-reduce.5.cloned.1.call-done = bf16[512,512]{1,0:T(8,128)(2,1)} async-done(((bf16[512,512]{1,0:T(8,128)(2,1)}), bf16[512,512]{1,0:T(8,128)(2,1)}) %all-reduce.5.cloned.1.call-update) | async-done | bytes 524304 | tf_op jit(solution)/shard_map/psum | solution.py:24
  114.6 1.2 convert_element_type.33
  115.9 0.2 multiply_reduce_fusion.1
  116.0 40.5 %all-reduce.1 = (f32[512]{0:T(512)S(1)}, f32[512]{0:T(512)S(1)}) all-reduce(f32[512]{0:T(512)S(1)} %multiply_reduce_fusion.1, f32[512]{0:T(512)S(1)} %multiply_reduce_fusion.2), channel_id=1, replica_groups=mesh['section'=8,'tp'=16] {'tp'}, use_global_device_ids=true, to_apply=%region_12.13 | all-reduce | flops 1024 | bytes 8192 | tf_op jit(solution)/shard_map/psum | solution.py:33
  156.6 1.3 multiply_convert_fusion.1
  157.9 0.5 all-gather.6.cloned.1.call-update
  159.1 0.1 fusion.2
  159.2 69.9 %all-gather.8.cloned.1.call-done = bf16[512,8192]{1,0:T(8,128)(2,1)} async-done(((bf16[512,512]{1,0:T(8,128)(2,1)}), bf16[512,8192]{1,0:T(8,128)(2,1)}) %all-gather.8.cloned.1.call-update) | async-done | bytes 8388624 | tf_op jit(solution)/shard_map/all_gather | solution.py:49
  229.1 14.8 %fusion.4 = (f32[512]{0:T(512)S(1)}, f32[512,1024]{1,0:T(8,128)S(1)}) fusion(bf16[512,8192]{1,0:T(8,128)(2,1)} %all-gather.8.cloned.1.call-done, bf16[8192,1024]{1,0:T(8,128)(2,1)} %param.12), kind=kOutput, calls=%fused_computation.31 | convolution fusion | flops 8590458880 | bytes 27265024 | tf_op jit(solution)/shard_map/dot_general | solution.py:48
  243.9 63.8 %all-gather.6.cloned.1.call-done = bf16[512,8192]{1,0:T(8,128)(2,1)} async-done(((bf16[512,512]{1,0:T(8,128)(2,1)}), bf16[512,8192]{1,0:T(8,128)(2,1)}) %all-gather.6.cloned.1.call-update) | async-done | bytes 8388624 | tf_op jit(solution)/shard_map/all_gather | solution.py:44
  307.7 16.0 %fusion.1 = (f32[512]{0:T(512)S(1)}, f32[512]{0:T(512)S(1)}, f32[512,1024]{1,0:T(8,128)}) fusion(s32[512]{0:T(512)S(1)} %add_subtract_fusion, bf16[512,8192]{1,0:T(8,128)(2,1)} %all-gather.6.cloned.1.call-done, bf16[8192,1024]{1,0:T(8,128)(2,1)} %param.12), kind=kOutput, calls=%fused_computation.28 | convolution fusion | flops 8592031744 | bytes 27269120 | tf_op jit(solution)/shard_map/dot_general | solution.py:43
  323.7 38.1 %all-reduce.2 = (f32[512]{0:T(512)S(1)}, f32[512]{0:T(512)S(1)}) all-reduce(f32[512]{0:T(512)S(1)} %get-tuple-element.70, f32[512]{0:T(512)S(1)} %get-tuple-element.32), channel_id=1, replica_groups=mesh['section'=8,'tp'=16] {'tp'}, use_global_device_ids=true, to_apply=%region_14.15 | all-reduce | flops 1024 | bytes 8192 | tf_op jit(solution)/shard_map/pmax | solution.py:57
  361.8 2.7 multiply_reduce_fusion
  364.5 35.9 %all-reduce = (f32[512]{0:T(512)S(1)}, f32[512]{0:T(512)S(1)}, f32[512]{0:T(512)S(1)}, f32[512]{0:T(512)S(1)}) all-reduce(f32[512]{0:T(512)S(1)} %get-tuple-element.30, f32[512]{0:T(512)S(1)} %get-tuple-element.29, f32[512]{0:T(512)S(1)} %get-tuple-element.33, f32[512]{0:T(512)S(1)} %get-tuple-element.31), channel_id=1, replica_groups=mesh['section'=8,'tp'=16] {'tp'}, use_global_device_ids=true, to_apply=%region_18.19 | all-reduce | flops 2048 | bytes 16384 | tf_op jit(solution)/shard_map/psum | solution.py:61
  400.5 0.7 bitcast_select_fusion
  (19 shorter events, 0.3 us)
Async XLA Ops:
  6.5 37.1 %all-gather.4.cloned.1.call-start = ((), (), s32[]{:S(2)}) async-start(), calls=%async_computation | async-start | bytes 4718592 | tf_op jit(solution)/shard_map/all_gather | solution.py:13
  7.3 107.4 %all-reduce.5.cloned.1.call-start = ((), (), s32[]{:S(2)}) async-start(), calls=%async_computation.2 | async-start | bytes 1048576 | tf_op jit(solution)/shard_map/psum | solution.py:24
  43.8 1.0 copy-start
  43.8 1.3 copy-start.1
  45.1 1.1 copy-start.2
  46.2 182.9 %all-gather.8.cloned.1.call-start = ((), (), s32[]{:S(2)}) async-start(), calls=%async_computation.3 | async-start | bytes 8912896 | tf_op jit(solution)/shard_map/all_gather | solution.py:49
  49.8 106.8 %copy-start.4 = (f32[512]{0:T(512)S(1)}, f32[512]{0:T(512)}, u32[]{:S(2)}) copy-start(f32[512]{0:T(512)} %param.11) | copy-start | bytes 6148
  156.6 2.5 copy-start.3
  157.9 149.8 %all-gather.6.cloned.1.call-start = ((), (), s32[]{:S(2)}) async-start(), calls=%async_computation.1 | async-start | bytes 8912896 | tf_op jit(solution)/shard_map/all_gather | solution.py:44
Sparse Core Ops, SparseCore 0:
  9.0 34.5 all-gather.3
  46.3 68.2 all-reduce.4
  158.0 71.0 all-gather.7
  231.1 76.6 all-gather.5
where the time goes:
time: 408 us
  waiting for transfers between devices  236 us (58%)
  blocking collectives  115 us (28%)
  matrix products  30.8 us (8%)
  between operations  16.5 us (4%)
  other arithmetic  7.16 us (2%)
    all_gather x1, waiting for transfers between devices, row_losses(): lax.all_gather(normed_teach, 'tp', axis=1, tiled=True)  69.9 us
    psum x1, waiting for transfers between devices, from_root(): return lax.psum(jnp.where(mine, shard, jnp.zeros_like(shard)), axis)  64.8 us
    all_gather x1, waiting for transfers between devices, row_losses(): lax.all_gather(normed_exit, 'tp', axis=1, tiled=True)  63.8 us
    psum x1, blocking collectives, row_losses(): lax.psum((jnp.sum(exit_rows * exit_rows, axis=1), jnp.sum(teach_rows * te...  40.5 us
    pmax x1, blocking collectives, row_losses(): lax.pmax((jnp.max(logit_exit, axis=1), jnp.max(logit_teach, axis=1)), 'tp')  38.1 us
    all_gather x1, waiting for transfers between devices, prefix(): gathered = lax.all_gather(shard.astype(jnp.bfloat16), axis)  36.3 us
    psum x1, blocking collectives, row_losses(): lax.psum((jnp.sum(jnp.exp(logit_exit - peak_exit[:, None]), axis=1), jnp....  35.9 us
    dot_general x1, matrix products, row_losses(): jnp.dot(lax.all_gather(normed_exit, 'tp', axis=1, tiled=True), out_embed,...  16 us
  transfers between devices with their start and end apart: 4, of which 4 were waited for; matrix products, arithmetic and copies ran while one was open for 4% of the time, Pallas kernels for 0%

commit v1 on v0

--- a/solution.py
+++ b/solution.py
@@ -21,7 +21,7 @@
 
 def from_root(shard, axis, root):
     mine = lax.axis_index(axis) == root
-    return lax.psum(jnp.where(mine, shard, jnp.zeros_like(shard)), axis)
+    return jnp.sum(lax.all_gather(jnp.where(mine, shard, jnp.zeros_like(shard)), axis), axis=0)
 
 
 def add_terms(first, second):

time: 408 us -> 382 us (0.936)
  waiting for transfers between devices: 236 us -> 208 us
    psum x1 -> x0, waiting for transfers between devices: 64.8 us -> none  [from_root(): return lax.psum(jnp.where(mine, shard, jnp.zeros_like(shard)), axis)]
    all_gather x0 -> x1, waiting for transfers between devices: none -> 36 us  [from_root(): lax.all_gather(jnp.where(mine, shard, jnp.zeros_like(shard)), axis)]
where the time goes in v1:
time: 382 us
  waiting for transfers between devices  208 us (54%)
  blocking collectives  115 us (30%)
  matrix products  30.8 us (8%)
  between operations  16.4 us (4%)
  other arithmetic  9.18 us (2%)
    all_gather x1, waiting for transfers between devices, row_losses(): lax.all_gather(normed_teach, 'tp', axis=1, tiled=True)  71.1 us
    all_gather x1, waiting for transfers between devices, row_losses(): lax.all_gather(normed_exit, 'tp', axis=1, tiled=True)  63.8 us
    psum x1, blocking collectives, row_losses(): lax.psum((jnp.sum(exit_rows * exit_rows, axis=1), jnp.sum(teach_rows * te...  40.5 us
    pmax x1, blocking collectives, row_losses(): lax.pmax((jnp.max(logit_exit, axis=1), jnp.max(logit_teach, axis=1)), 'tp')  38.1 us
    all_gather x1, waiting for transfers between devices, prefix(): gathered = lax.all_gather(shard.astype(jnp.bfloat16), axis)  36.3 us
    all_gather x1, waiting for transfers between devices, from_root(): lax.all_gather(jnp.where(mine, shard, jnp.zeros_like(shard)), axis)  36 us
    psum x1, blocking collectives, row_losses(): lax.psum((jnp.sum(jnp.exp(logit_exit - peak_exit[:, None]), axis=1), jnp....  35.9 us
    dot_general x1, matrix products, row_losses(): jnp.dot(lax.all_gather(normed_exit, 'tp', axis=1, tiled=True), out_embed,...  16 us
  transfers between devices with their start and end apart: 4, of which 4 were waited for; matrix products, arithmetic and copies ran while one was open for 4% of the time, Pallas kernels for 0%

profile of v1, /device:TPU:0, one launch (start us, length us, event | category | flops | bytes accessed | tf_op | source)
XLA Modules:
  0.0 381.9 jit_solution(7774481835155439892)
XLA Ops:
  6.5 0.7 all-gather.6.cloned.1.call-update
  7.3 36.3 %all-gather.6.cloned.1.call-done = bf16[8,512,512]{2,1,0:T(8,128)(2,1)} async-done(((bf16[1,512,512]{2,1,0:T(8,128)(2,1)}), bf16[8,512,512]{2,1,0:T(8,128)(2,1)}) %all-gather.6.cloned.1.call-update) | async-done | bytes 4194320 | tf_op jit(solution)/shard_map/all_gather | solution.py:13
  43.6 0.1 broadcast_in_dim.21
  43.8 1.0 copy-done
  44.8 0.3 copy-done.1
  45.1 1.0 convert_select_fusion
  46.2 0.6 fusion.3
  49.4 0.2 multiply_reduce_fusion.2
  49.6 36.0 %all-gather.12.cloned.1.call-done = bf16[4096,512]{1,0:T(8,128)(2,1)} async-done(((bf16[512,512]{1,0:T(8,128)(2,1)}), bf16[4096,512]{1,0:T(8,128)(2,1)}) %all-gather.12.cloned.1.call-update) | async-done | bytes 4194320 | tf_op jit(solution)/shard_map/all_gather | solution.py:24
  85.6 3.1 reduce_sum.69
  88.7 0.1 convert_element_type.35
  88.9 0.2 multiply_reduce_fusion.1
  89.1 40.5 %all-reduce.1 = (f32[512]{0:T(512)S(1)}, f32[512]{0:T(512)S(1)}) all-reduce(f32[512]{0:T(512)S(1)} %multiply_reduce_fusion.1, f32[512]{0:T(512)S(1)} %multiply_reduce_fusion.2), channel_id=1, replica_groups=mesh['section'=8,'tp'=16] {'tp'}, use_global_device_ids=true, to_apply=%region_12.13 | all-reduce | flops 1024 | bytes 8192 | tf_op jit(solution)/shard_map/psum | solution.py:33
  129.6 1.3 multiply_convert_fusion.1
  130.9 0.5 all-gather.8.cloned.1.call-update
  132.1 0.1 fusion.2
  132.2 71.1 %all-gather.10.cloned.1.call-done = bf16[512,8192]{1,0:T(8,128)(2,1)} async-done(((bf16[512,512]{1,0:T(8,128)(2,1)}), bf16[512,8192]{1,0:T(8,128)(2,1)}) %all-gather.10.cloned.1.call-update) | async-done | bytes 8388624 | tf_op jit(solution)/shard_map/all_gather | solution.py:49
  203.3 14.8 %fusion.4 = (f32[512]{0:T(512)S(1)}, f32[512,1024]{1,0:T(8,128)S(1)}) fusion(bf16[512,8192]{1,0:T(8,128)(2,1)} %all-gather.10.cloned.1.call-done, bf16[8192,1024]{1,0:T(8,128)(2,1)} %param.12), kind=kOutput, calls=%fused_computation.31 | convolution fusion | flops 8590458880 | bytes 27265024 | tf_op jit(solution)/shard_map/dot_general | solution.py:48
  218.2 63.8 %all-gather.8.cloned.1.call-done = bf16[512,8192]{1,0:T(8,128)(2,1)} async-done(((bf16[512,512]{1,0:T(8,128)(2,1)}), bf16[512,8192]{1,0:T(8,128)(2,1)}) %all-gather.8.cloned.1.call-update) | async-done | bytes 8388624 | tf_op jit(solution)/shard_map/all_gather | solution.py:44
  281.9 16.0 %fusion.1 = (f32[512]{0:T(512)S(1)}, f32[512]{0:T(512)S(1)}, f32[512,1024]{1,0:T(8,128)}) fusion(s32[512]{0:T(512)S(1)} %add_subtract_fusion, bf16[512,8192]{1,0:T(8,128)(2,1)} %all-gather.8.cloned.1.call-done, bf16[8192,1024]{1,0:T(8,128)(2,1)} %param.12), kind=kOutput, calls=%fused_computation.28 | convolution fusion | flops 8592031744 | bytes 27269120 | tf_op jit(solution)/shard_map/dot_general | solution.py:43
  297.9 38.1 %all-reduce.2 = (f32[512]{0:T(512)S(1)}, f32[512]{0:T(512)S(1)}) all-reduce(f32[512]{0:T(512)S(1)} %get-tuple-element.70, f32[512]{0:T(512)S(1)} %get-tuple-element.32), channel_id=1, replica_groups=mesh['section'=8,'tp'=16] {'tp'}, use_global_device_ids=true, to_apply=%region_14.15 | all-reduce | flops 1024 | bytes 8192 | tf_op jit(solution)/shard_map/pmax | solution.py:57
  336.1 2.7 multiply_reduce_fusion
  338.8 35.9 %all-reduce = (f32[512]{0:T(512)S(1)}, f32[512]{0:T(512)S(1)}, f32[512]{0:T(512)S(1)}, f32[512]{0:T(512)S(1)}) all-reduce(f32[512]{0:T(512)S(1)} %get-tuple-element.30, f32[512]{0:T(512)S(1)} %get-tuple-element.29, f32[512]{0:T(512)S(1)} %get-tuple-element.33, f32[512]{0:T(512)S(1)} %get-tuple-element.31), channel_id=1, replica_groups=mesh['section'=8,'tp'=16] {'tp'}, use_global_device_ids=true, to_apply=%region_18.19 | all-reduce | flops 2048 | bytes 16384 | tf_op jit(solution)/shard_map/psum | solution.py:61
  374.7 0.7 bitcast_select_fusion
  (20 shorter events, 0.4 us)
Async XLA Ops:
  6.5 37.1 %all-gather.6.cloned.1.call-start = ((), (), s32[]{:S(2)}) async-start(), calls=%async_computation | async-start | bytes 4718592 | tf_op jit(solution)/shard_map/all_gather | solution.py:13
  7.3 78.3 %all-gather.12.cloned.1.call-start = ((), (), s32[]{:S(2)}) async-start(), calls=%async_computation.3 | async-start | bytes 4718592 | tf_op jit(solution)/shard_map/all_gather | solution.py:24
  43.8 1.0 copy-start
  43.8 1.3 copy-start.1
  43.8 2.4 copy-start.2
  46.2 157.2 %all-gather.10.cloned.1.call-start = ((), (), s32[]{:S(2)}) async-start(), calls=%async_computation.2 | async-start | bytes 8912896 | tf_op jit(solution)/shard_map/all_gather | solution.py:49
  85.6 44.0 %copy-start.4 = (f32[512]{0:T(512)S(1)}, f32[512]{0:T(512)}, u32[]{:S(2)}) copy-start(f32[512]{0:T(512)} %param.11) | copy-start | bytes 6148
  88.7 43.5 %copy-start.3 = (s32[512]{0:T(512)S(1)}, s32[512]{0:T(512)}, u32[]{:S(2)}) copy-start(s32[512]{0:T(512)} %param.15) | copy-start | bytes 6148
  130.9 151.1 %all-gather.8.cloned.1.call-start = ((), (), s32[]{:S(2)}) async-start(), calls=%async_computation.1 | async-start | bytes 8912896 | tf_op jit(solution)/shard_map/all_gather | solution.py:44
Sparse Core Ops, SparseCore 0:
  9.0 34.5 all-gather.5
  46.3 39.2 all-gather.11
  131.0 72.2 all-gather.9
  205.3 76.6 all-gather.7

commit v2 on v0

--- a/solution.py
+++ b/solution.py
@@ -41,7 +41,9 @@
     ).astype(jnp.bfloat16)
     vocab_part = out_embed.shape[1]
     logit_exit = jnp.dot(
-        lax.all_gather(normed_exit, "tp", axis=1, tiled=True),
+        jnp.concatenate(
+            lax.all_to_all(jnp.stack([normed_exit] * lax.axis_size("tp")), "tp", 0, 0), axis=1
+        ),
         out_embed,
         preferred_element_type=jnp.float32,
     )

time: 408 us -> 422 us (1.034)
  starting transfers between devices: 0.12 us -> 5.01 us
  local copies, waits for them, and re-layouts: 2.36 us -> 6.6 us
    all_to_all x0 -> x1, waiting for transfers between devices: none -> 103 us  [row_losses(): lax.all_to_all(jnp.stack([normed_exit] * lax.axis_size('tp')), 'tp', 0, 0)]
    all_gather x1 -> x0, waiting for transfers between devices: 63.8 us -> none  [row_losses(): lax.all_gather(normed_exit, 'tp', axis=1, tiled=True)]
    all_gather x1, waiting for transfers between devices: 69.9 us -> 34.8 us  [row_losses(): lax.all_gather(normed_teach, 'tp', axis=1, tiled=True)]
    all_to_all x0 -> x1, starting transfers between devices: none -> 4.93 us  [row_losses(): lax.all_to_all(jnp.stack([normed_exit] * lax.axis_size('tp')), 'tp', 0, 0)]
  transfers between devices with their start and end apart: 4 -> 4, of which waited for: 4 -> 4; matrix products, arithmetic and copies ran while one was open for 4% -> 5% of each run, Pallas kernels for 0% -> 0%
where the time goes in v2:
time: 422 us; the launch traced here: 421 us
  waiting for transfers between devices  240 us (57%)
  blocking collectives  115 us (27%)
  matrix products  31.5 us (7%)
  between operations  16.5 us (4%)
  other arithmetic  6.98 us (2%)
  local copies, waits for them, and re-layouts  6.6 us (2%)
  starting transfers between devices  5.01 us (1%)
    all_to_all x1, waiting for transfers between devices, row_losses(): lax.all_to_all(jnp.stack([normed_exit] * lax.axis_size('tp')), 'tp', 0, 0)  103 us
    psum x1, waiting for transfers between devices, from_root(): return lax.psum(jnp.where(mine, shard, jnp.zeros_like(shard)), axis)  64.9 us
    psum x1, blocking collectives, row_losses(): lax.psum((jnp.sum(exit_rows * exit_rows, axis=1), jnp.sum(teach_rows * te...  40.5 us
    pmax x1, blocking collectives, row_losses(): lax.pmax((jnp.max(logit_exit, axis=1), jnp.max(logit_teach, axis=1)), 'tp')  38.1 us
    all_gather x1, waiting for transfers between devices, prefix(): gathered = lax.all_gather(shard.astype(jnp.bfloat16), axis)  36.3 us
    psum x1, blocking collectives, row_losses(): lax.psum((jnp.sum(jnp.exp(logit_exit - peak_exit[:, None]), axis=1), jnp....  35.9 us
    all_gather x1, waiting for transfers between devices, row_losses(): lax.all_gather(normed_teach, 'tp', axis=1, tiled=True)  34.8 us
    dot_general x1, matrix products, row_losses(): jnp.dot(lax.all_gather(normed_teach, 'tp', axis=1, tiled=True), out_embed...  16 us
  transfers between devices with their start and end apart: 4, of which 4 were waited for; matrix products, arithmetic and copies ran while one was open for 5% of the time, Pallas kernels for 0%

profile of v2, /device:TPU:0, one launch (start us, length us, event | category | flops | bytes accessed | tf_op | source)
XLA Modules:
  0.0 421.4 jit_solution(7865122768724224138)
XLA Ops:
  6.5 0.7 all-gather.3.cloned.1.call-update
  7.3 36.3 %all-gather.3.cloned.1.call-done = bf16[8,512,512]{2,1,0:T(8,128)(2,1)} async-done(((bf16[1,512,512]{2,1,0:T(8,128)(2,1)}), bf16[8,512,512]{2,1,0:T(8,128)(2,1)}) %all-gather.3.cloned.1.call-update) | async-done | bytes 4194320 | tf_op jit(solution)/shard_map/all_gather | solution.py:13
  43.6 0.1 broadcast_in_dim.21
  43.8 1.0 copy-done
  44.8 0.3 copy-done.1
  45.1 1.1 convert_select_fusion
  46.2 0.7 fusion.3
  49.6 0.1 multiply_reduce_fusion.2
  49.8 64.9 %all-reduce.5.cloned.1.call-done = bf16[512,512]{1,0:T(8,128)(2,1)} async-done(((bf16[512,512]{1,0:T(8,128)(2,1)}), bf16[512,512]{1,0:T(8,128)(2,1)}) %all-reduce.5.cloned.1.call-update) | async-done | bytes 524304 | tf_op jit(solution)/shard_map/psum | solution.py:24
  114.7 1.2 convert_element_type.35
  116.0 0.2 multiply_reduce_fusion.1
  116.1 40.5 %all-reduce.1 = (f32[512]{0:T(512)S(1)}, f32[512]{0:T(512)S(1)}) all-reduce(f32[512]{0:T(512)S(1)} %multiply_reduce_fusion.1, f32[512]{0:T(512)S(1)} %multiply_reduce_fusion.2), channel_id=1, replica_groups=mesh['section'=8,'tp'=16] {'tp'}, use_global_device_ids=true, to_apply=%region_12.13 | all-reduce | flops 1024 | bytes 8192 | tf_op jit(solution)/shard_map/psum | solution.py:33
  156.7 1.1 multiply_convert_fusion.1
  157.8 0.2 copy.9
  158.0 4.0 stack.2
  162.0 4.9 %all-to-all-start = ((bf16[16,512,512]{1,2,0:T(8,128)(2,1)}), bf16[16,512,512]{1,2,0:T(8,128)(2,1)}, u32[]{:S(2)}, u32[]{:S(2)}) async-start(bf16[16,512,512]{1,2,0:T(8,128)(2,1)} %stack.2), calls=%async_computation | async-start | bytes 16777216 | tf_op jit(solution)/shard_map/all_to_all | solution.py:45
  167.7 103.4 %all-to-all-done = bf16[16,512,512]{1,2,0:T(8,128)(2,1)} async-done(((bf16[16,512,512]{1,2,0:T(8,128)(2,1)}), bf16[16,512,512]{1,2,0:T(8,128)(2,1)}, u32[]{:S(2)}, u32[]{:S(2)}) %all-to-all-start) | async-done | bytes 8388640 | tf_op jit(solution)/shard_map/all_to_all | solution.py:45
  271.1 15.6 %fusion.1 = (f32[512]{0:T(512)S(1)}, f32[512]{0:T(512)S(1)}, f32[512,1024]{1,0:T(8,128)S(1)}) fusion(s32[512]{0:T(512)S(1)} %add_subtract_fusion, bf16[512,8192]{0,1:T(8,128)(2,1)} %bitcast.8, bf16[8192,1024]{1,0:T(8,128)(2,1)} %param.12), kind=kOutput, calls=%fused_computation.28 | convolution fusion | flops 8592031744 | bytes 27269120 | tf_op jit(solution)/shard_map/dot_general | solution.py:43
  286.7 34.8 %all-gather.5.cloned.1.call-done = bf16[512,8192]{1,0:T(8,128)(2,1)} async-done(((bf16[512,512]{1,0:T(8,128)(2,1)}), bf16[512,8192]{1,0:T(8,128)(2,1)}) %all-gather.5.cloned.1.call-update) | async-done | bytes 8388624 | tf_op jit(solution)/shard_map/all_gather | solution.py:51
  321.5 16.0 %fusion.4 = (f32[512]{0:T(512)S(1)}, f32[512,1024]{1,0:T(8,128)}) fusion(bf16[512,8192]{1,0:T(8,128)(2,1)} %all-gather.5.cloned.1.call-done, bf16[8192,1024]{1,0:T(8,128)(2,1)} %param.12), kind=kOutput, calls=%fused_computation.31 | convolution fusion | flops 8590458880 | bytes 27265024 | tf_op jit(solution)/shard_map/dot_general | solution.py:50
  337.5 38.1 %all-reduce.2 = (f32[512]{0:T(512)S(1)}, f32[512]{0:T(512)S(1)}) all-reduce(f32[512]{0:T(512)S(1)} %get-tuple-element.70, f32[512]{0:T(512)S(1)} %get-tuple-element.32), channel_id=1, replica_groups=mesh['section'=8,'tp'=16] {'tp'}, use_global_device_ids=true, to_apply=%region_14.15 | all-reduce | flops 1024 | bytes 8192 | tf_op jit(solution)/shard_map/pmax | solution.py:59
  375.6 2.7 multiply_reduce_fusion
  378.3 35.9 %all-reduce = (f32[512]{0:T(512)S(1)}, f32[512]{0:T(512)S(1)}, f32[512]{0:T(512)S(1)}, f32[512]{0:T(512)S(1)}) all-reduce(f32[512]{0:T(512)S(1)} %get-tuple-element.30, f32[512]{0:T(512)S(1)} %get-tuple-element.29, f32[512]{0:T(512)S(1)} %get-tuple-element.33, f32[512]{0:T(512)S(1)} %get-tuple-element.31), channel_id=1, replica_groups=mesh['section'=8,'tp'=16] {'tp'}, use_global_device_ids=true, to_apply=%region_18.19 | all-reduce | flops 2048 | bytes 16384 | tf_op jit(solution)/shard_map/psum | solution.py:63
  414.3 0.7 bitcast_select_fusion
  (20 shorter events, 0.4 us)
Async XLA Ops:
  6.5 37.1 %all-gather.3.cloned.1.call-start = ((), (), s32[]{:S(2)}) async-start(), calls=%async_computation.1 | async-start | bytes 4718592 | tf_op jit(solution)/shard_map/all_gather | solution.py:13
  7.3 107.4 %all-reduce.5.cloned.1.call-start = ((), (), s32[]{:S(2)}) async-start(), calls=%async_computation.2 | async-start | bytes 1048576 | tf_op jit(solution)/shard_map/psum | solution.py:24
  43.8 1.0 copy-start
  43.8 1.3 copy-start.1
  43.8 2.4 copy-start.2
  46.2 110.5 %copy-start.4 = (f32[512]{0:T(512)S(1)}, f32[512]{0:T(512)}, u32[]{:S(2)}) copy-start(f32[512]{0:T(512)} %param.11) | copy-start | bytes 6148
  46.2 275.3 %all-gather.5.cloned.1.call-start = ((), (), s32[]{:S(2)}) async-start(), calls=%async_computation.3 | async-start | bytes 8912896 | tf_op jit(solution)/shard_map/all_gather | solution.py:51
  162.0 5.6 %copy-start.3 = (s32[512]{0:T(512)S(1)}, s32[512]{0:T(512)}, u32[]{:S(2)}) copy-start(s32[512]{0:T(512)} %param.15) | copy-start | bytes 6148
  162.0 109.1 %all-to-all-start = ((bf16[16,512,512]{1,2,0:T(8,128)(2,1)}), bf16[16,512,512]{1,2,0:T(8,128)(2,1)}, u32[]{:S(2)}, u32[]{:S(2)}) async-start(bf16[16,512,512]{1,2,0:T(8,128)(2,1)} %stack.2), calls=%async_computation | async-start | bytes 16777216 | tf_op jit(solution)/shard_map/all_to_all | solution.py:45
Sparse Core Ops, SparseCore 0:
  9.0 34.5 all-gather.2
  46.3 68.3 all-reduce.4
  157.9 163.5 all-gather.4
